TPU v7x, 32 devices: a whole 2x2x4 slice. The times are simulated.
32 devices in a mesh: row: 8 (over z, y), col: 4 (over x, core).
Axes of the slice: x: 2, y: 2, z: 4, core: 2. Of those that a mesh axis runs over, the one named last changes fastest.
Arguments:
- anc_inverse: float32 [20480, 20480], P('row', 'col'), may hold values from -6 to 6
- l_store: float32 [4, 20480, 256], P('col', 'row'), may hold values from -0.0546875 to 0.0546875
- diag_inv: float32 [4, 256, 256], P('col'), may hold values from -6 to 6
- block_lists: int32 [4, 96], replicated, may hold values from 0 to 159, as said below
- block_counts: int32 [4], replicated, may hold values from 48 to 96, as said below
- sibling_columns: int32 [4], replicated, may hold values from 0 to 3, as said below
Outputs:
- upper_out: float32 [4, 256, 20480], P(None, 'row', 'col')
- lower_out: float32 [4, 20480, 256], P('col', 'row')
- diag_out: float32 [4, 256, 256], P('col')
Inputs may be any that keep to these rules, and one draw needn't show every extreme that they name: `block_lists`: in each sibling's row the entries are distinct block indices; entries at positions from block_counts onward are ignored. `block_counts`: some sibling uses all 96 entries. `sibling_columns`: distinct columns for distinct siblings.
All inputs are finite; a program needn't handle non-finite values.
Results may differ from a plain program's by a relative error of at most 0.00011.
Values sent between devices are 32-bit elements; how exact they have to be, the bound alone decides.
A program may use at most 128 MiB of HBM per device.

v0:
```python
import functools

import jax
import jax.numpy as jnp
from jax import lax
from jax.experimental import pallas as pl
from jax.experimental.pallas import tpu as pltpu
from jax.sharding import PartitionSpec as P

BLK = 128
GROUP = 4
MESH = pl.DeviceIdType.MESH


def listed_table(block_lists, block_counts, block_total):
    block_ids = jnp.arange(block_total, dtype=jnp.int32)
    valid_entry = jnp.arange(block_lists.shape[1], dtype=jnp.int32)[None, :] < block_counts[:, None]
    entry_hits = (block_lists[:, :, None] == block_ids[None, None, :]) & valid_entry[:, :, None]
    return jnp.any(entry_hits, axis=1)


def product_kernel(members, tile_blocks, col_blocks, row_blocks, joins, saved,
                   slot_ref, rows_ref, count_ref, a_ref, *refs):
    panel_refs, refs = refs[:members], refs[members:]
    if joins:
        _, kept_high, kept_low, out_ref, highs, lows, p_high, p_low, stage, sent, kept = refs
    else:
        out_ref, kept_high, kept_low, highs, lows, p_high, p_low, stage, sent, kept = refs
    step, stripes = pl.program_id(0), pl.num_programs(0)
    split = stripes - saved

    def stripe_at(at):
        return jnp.where(at < split, saved + at, at - split) if joins else at

    stripe = stripe_at(step)
    side = lax.rem(step, 2) if joins else 0
    a_high, a_low = highs.at[side], lows.at[side]
    group = p_high.shape[3] // BLK
    listed = p_high.shape[1] * group

    def keep_copies(at):
        return (
            pltpu.make_async_copy(highs.at[0], kept_high.at[at], kept.at[0, 0]),
            pltpu.make_async_copy(lows.at[0], kept_low.at[at], kept.at[0, 1]),
        )

    def load_copies(at):
        to = lax.rem(at, 2)
        return (
            pltpu.make_async_copy(kept_high.at[at - split], highs.at[to], kept.at[to, 0]),
            pltpu.make_async_copy(kept_low.at[at - split], lows.at[to], kept.at[to, 1]),
        )

    @pl.when(step == 0)
    def _():
        for member in range(members):
            @pl.loop(0, count_ref[member])
            def _(i):
                rows = pl.ds(pl.multiple_of(rows_ref[member * listed + i] * BLK, BLK), BLK)
                lanes = pl.ds(pl.multiple_of(lax.rem(i, group) * BLK, BLK), BLK)
                value = -panel_refs[member][rows, :].T
                high = value.astype(jnp.bfloat16)
                p_high[member, i // group, :, lanes] = high
                p_low[member, i // group, :, lanes] = (value - high.astype(jnp.float32)).astype(jnp.bfloat16)

            @pl.loop(count_ref[member], (count_ref[member] + group - 1) // group * group)
            def _(i):
                lanes = pl.ds(pl.multiple_of(lax.rem(i, group) * BLK, BLK), BLK)
                zero = jnp.zeros((p_high.shape[2], BLK), jnp.bfloat16)
                p_high[member, i // group, :, lanes] = zero
                p_low[member, i // group, :, lanes] = zero

    def halve():
        @pl.loop(0, row_blocks)
        def _(block):
            rows = pl.ds(pl.multiple_of(block * BLK, BLK), BLK)
            value = a_ref[rows, :]
            high = value.astype(jnp.bfloat16)
            a_high[block] = high
            a_low[block] = (value - high.astype(jnp.float32)).astype(jnp.bfloat16)

    if joins:
        @pl.when((step + 1 >= split) & (step + 1 < stripes))
        def _():
            for copy in load_copies(step + 1):
                copy.start()

        pl.when(step < split)(halve)

        @pl.when(step >= split)
        def _():
            for copy in load_copies(step):
                copy.wait()
    else:
        @pl.when((step > 0) & (step <= saved))
        def _():
            for copy in keep_copies(step - 1):
                copy.wait()

        halve()

        @pl.when(step < saved)
        def _():
            for copy in keep_copies(step):
                copy.start()

    def slot_of(member, block, at):
        return slot_ref[member * col_blocks + at * tile_blocks + block]

    def slot_copy(member, block, slot):
        return pltpu.make_async_copy(
            stage.at[member, :, pl.ds(block * BLK, BLK)],
            out_ref.at[:, pl.ds(pl.multiple_of(slot * BLK, BLK), BLK)],
            sent.at[member, block],
        )

    def settle(member, at):
        for block in range(tile_blocks):
            slot = slot_of(member, block, at)

            @pl.when(slot >= 0)
            def _():
                slot_copy(member, block, slot).wait()

    for member in range(members):
        @pl.when(step > 0)
        def _():
            settle(member, stripe_at(step - 1))

        stage[member] = jnp.zeros(stage.shape[1:], jnp.float32)

        def add(k, blocks):
            at = [rows_ref[member * listed + k * group + u] for u in range(blocks)]
            part = slice(0, blocks * BLK)
            ph, plo = p_high[member, k, :, part], p_low[member, k, :, part]
            ah, al = [a_high[i] for i in at], [a_low[i] for i in at]
            left = jnp.concatenate([ph, ph, plo], axis=1)
            right = jnp.concatenate(ah + al + ah, axis=0)
            stage[member] += jnp.dot(left, right, preferred_element_type=jnp.float32)

        short = group // 2
        whole = (count_ref[member] + short - 1) // group

        @pl.loop(0, whole)
        def _(k):
            add(k, group)

        @pl.when(count_ref[member] > whole * group)
        def _():
            add(whole, short)

        for block in range(tile_blocks):
            slot = slot_of(member, block, stripe)

            @pl.when(slot >= 0)
            def _():
                slot_copy(member, block, slot).start()

    @pl.when(step == stripes - 1)
    def _():
        for member in range(members):
            settle(member, stripe)


def product(slot, rows, counts, anc, panels, slots_all, before=None):
    members = counts.shape[0]
    depth, cells = anc.shape
    width = panels[0].shape[1]
    row_blocks, col_blocks = depth // BLK, cells // BLK
    tile_blocks = next(n for n in (8, 4, 2, 1) if col_blocks % n == 0)
    tile = tile_blocks * BLK
    groups = rows.shape[1] // GROUP
    joins = () if before is None else tuple(before)
    stripes = col_blocks // tile_blocks
    saved = stripes - 1
    any_space = pl.BlockSpec(memory_space=pl.ANY)
    kept = jax.ShapeDtypeStruct((saved, row_blocks, BLK, tile), jnp.bfloat16)
    value = jax.ShapeDtypeStruct((width, slots_all * BLK), jnp.float32)
    sides = 2 if joins else 1
    first = saved if joins else 0
    held = pl.BlockSpec((depth, width), lambda i, *_: (0, 0), pipeline_mode=pl.Buffered(1))
    return pl.pallas_call(
        functools.partial(product_kernel, members, tile_blocks, col_blocks, row_blocks, len(joins), saved),
        out_shape=value if joins else (value, kept, kept),
        grid_spec=pltpu.PrefetchScalarGridSpec(
            num_scalar_prefetch=3,
            grid=(stripes,),
            in_specs=[pl.BlockSpec((depth, tile), lambda i, *_: (0, jnp.minimum(first + i, stripes - 1)))]
            + [held] * members
            + [any_space] * len(joins),
            out_specs=any_space if joins else (any_space,) * 3,
            scratch_shapes=[
                pltpu.VMEM((sides, row_blocks, BLK, tile), jnp.bfloat16),
                pltpu.VMEM((sides, row_blocks, BLK, tile), jnp.bfloat16),
                pltpu.VMEM((members, groups, width, GROUP * BLK), jnp.bfloat16),
                pltpu.VMEM((members, groups, width, GROUP * BLK), jnp.bfloat16),
                pltpu.VMEM((members, width, tile), jnp.float32),
                pltpu.SemaphoreType.DMA((members, tile_blocks)),
                pltpu.SemaphoreType.DMA((sides, 2)),
            ],
        ),
        input_output_aliases={4 + members: 0} if joins else {},
        cost_estimate=pl.CostEstimate(
            flops=2 * 3 * members * depth * cells * width // 2,
            bytes_accessed=4 * depth * cells + 4 * members * width * cells,
            transcendentals=0,
        ),
        compiler_params=pltpu.CompilerParams(
            dimension_semantics=("arbitrary",), vmem_limit_bytes=63 * 1024 * 1000
        ),
    )(slot.reshape(-1), rows.reshape(-1), counts, anc, *panels, *joins)


def expand_kernel(siblings, col_count, col_blocks, slot_ref, owner_ref, compact_ref, upper_ref, slots_ref):
    @pl.loop(0, col_blocks)
    def _(block):
        lanes = pl.ds(pl.multiple_of(block * BLK, BLK), BLK)
        for sibling in range(siblings):
            slot = slot_ref[sibling * col_blocks + block]
            at = pl.ds(pl.multiple_of(jnp.maximum(slot, 0) * BLK, BLK), BLK)
            value = compact_ref[:, at]
            upper_ref[sibling, :, lanes] = jnp.where(slot >= 0, value, jnp.zeros_like(value))

    for column in range(col_count):
        sibling = owner_ref[column]
        value = upper_ref[jnp.maximum(sibling, 0)]
        slots_ref[column] = jnp.where(sibling >= 0, value, jnp.zeros_like(value))


def expand(slot, owner, compact, siblings, col_blocks):
    col_count = owner.shape[0]
    rows = compact.shape[0]
    return pl.pallas_call(
        functools.partial(expand_kernel, siblings, col_count, col_blocks),
        out_shape=(
            jax.ShapeDtypeStruct((siblings, rows, col_blocks * BLK), jnp.float32),
            jax.ShapeDtypeStruct((col_count, rows, col_blocks * BLK), jnp.float32),
        ),
        in_specs=[pl.BlockSpec(memory_space=pltpu.SMEM)] * 2 + [pl.BlockSpec(memory_space=pltpu.VMEM)],
        out_specs=(pl.BlockSpec(memory_space=pltpu.VMEM),) * 2,
    )(slot, owner, compact)


def reduce_kernel(line, flat_first, chunks,
                  partial_ref, out_ref,
                  mine, flat_mine, pair_buf, up_buf, down_buf, flat_up, flat_down, flat_sum, flat_pair,
                  mine_sem, flat_sem, pair_send, pair_recv, up_send, up_recv, down_send, down_recv, flat_send, flat_recv):
    r, c = lax.axis_index("row"), lax.axis_index("col")
    z, y = r // 2, lax.rem(r, 2)
    other = 1 - y
    width = out_ref.shape[1] // chunks
    last, lag = line - 1, 2
    late = chunks - flat_first

    def lanes(chunk):
        return pl.ds(pl.multiple_of(chunk * width, width), width)

    def flat_load(k):
        return pltpu.make_async_copy(partial_ref.at[:, :, :, lanes(k)], flat_mine.at[k], flat_sem.at[k])

    def pair_load(k):
        return pltpu.make_async_copy(
            partial_ref.at[:, y, :, lanes(k + flat_first)], mine.at[k], mine_sem.at[k]
        )

    @pl.loop(0, flat_first)
    def _(k):
        flat_load(k).start()

    barrier = pltpu.get_barrier_semaphore()
    pl.semaphore_signal(barrier, inc=1, device_id=(z * 2 + other, c), device_id_type=MESH)

    @pl.when(z > 0)
    def _():
        pl.semaphore_signal(barrier, inc=1, device_id=(r - 2, c), device_id_type=MESH)

    @pl.when(z < last)
    def _():
        pl.semaphore_signal(barrier, inc=1, device_id=(r + 2, c), device_id_type=MESH)

    pl.semaphore_wait(barrier, 1 + (z > 0).astype(jnp.int32) + (z < last).astype(jnp.int32))

    def pair_copy(k):
        return pltpu.make_async_remote_copy(
            src_ref=partial_ref.at[:, other, :, lanes(k + flat_first)],
            dst_ref=pair_buf.at[k],
            send_sem=pair_send.at[k],
            recv_sem=pair_recv.at[k],
            device_id=(z * 2 + other, c),
            device_id_type=MESH,
        )

    def flat_copy(k):
        return pltpu.make_async_remote_copy(
            src_ref=flat_sum.at[k, other],
            dst_ref=flat_pair.at[k],
            send_sem=flat_send.at[k],
            recv_sem=flat_recv.at[k],
            device_id=(z * 2 + other, c),
            device_id_type=MESH,
        )

    def up_copy(buf, k, slot, at):
        return pltpu.make_async_remote_copy(
            src_ref=buf.at[k, pl.ds(at, last - at)],
            dst_ref=buf.at[k, pl.ds(at, last - at)],
            send_sem=up_send.at[slot],
            recv_sem=up_recv.at[slot],
            device_id=(r + 2, c),
            device_id_type=MESH,
        )

    def down_copy(buf, k, slot, at):
        return pltpu.make_async_remote_copy(
            src_ref=buf.at[k, pl.ds(0, at)],
            dst_ref=buf.at[k, pl.ds(0, at)],
            send_sem=down_send.at[slot],
            recv_sem=down_recv.at[slot],
            device_id=(r - 2, c),
            device_id_type=MESH,
        )

    def flat(k):
        def own(place):
            return flat_mine[k, place]

        def finish(value):
            flat_sum[k] = value
            flat_copy(k).start()

        return flat_up, flat_down, k, own, finish

    def paired(k):
        k = k - flat_first

        def own(place):
            return pair_buf[k, place]

        def finish(value):
            out_ref[:, lanes(k + flat_first)] = value

        return up_buf, down_buf, k, own, finish

    def total(at, up, down, k, own, finish):
        value = own(at)
        if at > 0:
            value = value + up[k, at - 1]
        if at < last:
            value = value + down[k, at]
        finish(value)

    def pass_up(at, slot, up, down, k, own, finish):
        if at > 0:
            up_copy(up, k, slot, at - 1).wait_recv()
        for place in range(at + 1, line):
            if at > 0:
                up[k, place - 1] = up[k, place - 1] + own(place)
            else:
                up[k, place - 1] = own(place)
        if at < last:
            up_copy(up, k, slot, at).start()
        if 2 * at > last:
            total(at, up, down, k, own, finish)

    def pass_down(at, slot, up, down, k, own, finish):
        if at < last:
            down_copy(down, k, slot, at + 1).wait_recv()
        for place in range(at):
            if at < last:
                down[k, place] = down[k, place] + own(place)
            else:
                down[k, place] = own(place)
        if at > 0:
            down_copy(down, k, slot, at).start()
        if 2 * at <= last:
            total(at, up, down, k, own, finish)

    def either(step, at, slot):
        @pl.when((slot >= 0) & (slot < flat_first))
        def _():
            step(at, slot, *flat(slot))

        @pl.when((slot >= flat_first) & (slot < chunks))
        def _():
            step(at, slot, *paired(slot))

    @pl.loop(0, late)
    def _(k):
        pair_copy(k).start()
        pair_load(k).start()

    @pl.loop(0, chunks + lag * last)
    def _(i):
        @pl.when(i < flat_first)
        def _():
            flat_load(i).wait()

        @pl.when((i >= flat_first) & (i < chunks))
        def _():
            k = i - flat_first
            pair_load(k).wait()
            pair_copy(k).wait_recv()
            for place in range(line):
                pair_buf[k, place] = pair_buf[k, place] + mine[k, place]

        for at in range(line):
            @pl.when(z == at)
            def _():
                either(pass_up, at, i - lag * at)
                either(pass_down, at, i - lag * (last - at))

    @pl.loop(0, flat_first)
    def _(k):
        flat_copy(k).wait_recv()
        out_ref[:, lanes(k)] = flat_sum[k, y] + flat_pair[k]

    @pl.loop(0, late)
    def _(k):
        pair_copy(k).wait_send()

    @pl.loop(0, flat_first)
    def _(k):
        flat_copy(k).wait_send()

    for at in range(line):
        @pl.when(z == at)
        def _():
            for buf, start, stop, shift in ((flat_up, 0, flat_first, 0), (up_buf, 0, late, flat_first)):
                if at < last:
                    @pl.loop(start, stop)
                    def _(k):
                        up_copy(buf, k, k + shift, at).wait_send()
            for buf, start, stop, shift in ((flat_down, 0, flat_first, 0), (down_buf, 0, late, flat_first)):
                if at > 0:
                    @pl.loop(start, stop)
                    def _(k):
                        down_copy(buf, k, k + shift, at).wait_send()


def reduce_rows(value, row_count, chunks, lanes, collective):
    width, columns = value.shape
    line, slice_rows = row_count // 2, width // row_count
    flat_first = (chunks + 3) // 6
    late = chunks - flat_first
    vmem = pl.BlockSpec(memory_space=pltpu.VMEM)
    dma = pltpu.SemaphoreType.DMA
    return pl.pallas_call(
        functools.partial(reduce_kernel, line, flat_first, chunks),
        out_shape=jax.ShapeDtypeStruct((slice_rows, chunks * lanes), jnp.float32),
        in_specs=[pl.BlockSpec(memory_space=pl.ANY)],
        out_specs=vmem,
        scratch_shapes=[
            pltpu.VMEM((late, line, slice_rows, lanes), jnp.float32),
            pltpu.VMEM((flat_first, line, 2, slice_rows, lanes), jnp.float32),
            pltpu.VMEM((late, line, slice_rows, lanes), jnp.float32),
            pltpu.VMEM((late, line - 1, slice_rows, lanes), jnp.float32),
            pltpu.VMEM((late, line - 1, slice_rows, lanes), jnp.float32),
            pltpu.VMEM((flat_first, line - 1, 2, slice_rows, lanes), jnp.float32),
            pltpu.VMEM((flat_first, line - 1, 2, slice_rows, lanes), jnp.float32),
            pltpu.VMEM((flat_first, 2, slice_rows, lanes), jnp.float32),
            pltpu.VMEM((flat_first, slice_rows, lanes), jnp.float32),
            dma((late,)),
            dma((flat_first,)),
            dma((late,)),
            dma((late,)),
            dma((chunks,)),
            dma((chunks,)),
            dma((chunks,)),
            dma((chunks,)),
            dma((flat_first,)),
            dma((flat_first,)),
        ],
        compiler_params=pltpu.CompilerParams(
            collective_id=collective, has_side_effects=True, vmem_limit_bytes=63 * 1024 * 1000
        ),
    )(value.reshape(line, 2, slice_rows, columns))


def finish_kernel(row_count, col_count,
                  owner_ref, slots_ref, own_ref, base_ref, lower_ref, diag_ref,
                  stage, picked, inner, part, reduced, total,
                  stage_send, stage_recv, send_sem, recv_sem, part_send, part_recv, total_send, total_recv):
    r, c = lax.axis_index("row"), lax.axis_index("col")
    ratio = row_count // col_count
    slice_rows, cells = picked.shape[1], picked.shape[2]

    barrier = pltpu.get_barrier_semaphore()
    for peer in range(row_count):
        @pl.when(peer != r)
        def _():
            pl.semaphore_signal(barrier, inc=1, device_id=(peer, c), device_id_type=MESH)
    for peer in range(col_count):
        @pl.when(peer != c)
        def _():
            pl.semaphore_signal(barrier, inc=1, device_id=(r, peer), device_id_type=MESH)
    pl.semaphore_wait(barrier, row_count + col_count - 2)

    def near(offset):
        pair = lax.rem(c // 2 + offset // 2, col_count // 2)
        return pair * 2 + lax.rem(lax.rem(c, 2) + offset % 2, 2)

    def piece(k):
        return pl.ds(k * cells, cells)

    def column_copy(target, k):
        return pltpu.make_async_remote_copy(
            src_ref=slots_ref.at[target, :, piece(k)],
            dst_ref=stage.at[c, :, piece(k)],
            send_sem=stage_send.at[target, k],
            recv_sem=stage_recv.at[c, k],
            device_id=(r, target),
            device_id_type=MESH,
        )

    def column_arrived(source, k):
        return pltpu.make_async_remote_copy(
            src_ref=slots_ref.at[source, :, piece(k)],
            dst_ref=stage.at[source, :, piece(k)],
            send_sem=stage_send.at[source, k],
            recv_sem=stage_recv.at[source, k],
            device_id=(r, source),
            device_id_type=MESH,
        )

    def row_copy(held, source, k):
        target = source * ratio + k
        return pltpu.make_async_remote_copy(
            src_ref=held.at[source, :, piece(k)],
            dst_ref=picked.at[r],
            send_sem=send_sem.at[target],
            recv_sem=recv_sem.at[r],
            device_id=(target, c),
            device_id_type=MESH,
        )

    def row_local(held, source, k):
        return pltpu.make_async_copy(
            held.at[source, :, piece(k)], picked.at[r], recv_sem.at[r]
        )

    def row_arrived(source):
        return pltpu.make_async_remote_copy(
            src_ref=picked.at[source],
            dst_ref=picked.at[source],
            send_sem=send_sem.at[source],
            recv_sem=recv_sem.at[source],
            device_id=(source, c),
            device_id_type=MESH,
        )

    for offset in (*range(2, col_count), 1):
        for k in range(ratio):
            column_copy(near(offset), k).start()
    for offset in range(col_count):
        source = near(offset)
        held = stage if offset else slots_ref
        for k in range(ratio):
            if offset:
                column_arrived(source, k).wait_recv()

            @pl.when(source * ratio + k == r)
            def _():
                row_local(held, source, k).start()

            @pl.when(source * ratio + k != r)
            def _():
                row_copy(held, source, k).start()

    def part_copy(peer):
        return pltpu.make_async_remote_copy(
            src_ref=inner.at[pl.ds(pl.multiple_of(peer * slice_rows, slice_rows), slice_rows), :],
            dst_ref=part.at[r],
            send_sem=part_send.at[peer],
            recv_sem=part_recv.at[r],
            device_id=(peer, c),
            device_id_type=MESH,
        )

    def part_arrived(peer):
        return pltpu.make_async_remote_copy(
            src_ref=inner.at[pl.ds(0, slice_rows), :],
            dst_ref=part.at[peer],
            send_sem=part_send.at[peer],
            recv_sem=part_recv.at[peer],
            device_id=(peer, c),
            device_id_type=MESH,
        )

    def total_copy(peer):
        return pltpu.make_async_remote_copy(
            src_ref=reduced,
            dst_ref=total.at[r],
            send_sem=total_send.at[peer],
            recv_sem=total_recv.at[r],
            device_id=(peer, c),
            device_id_type=MESH,
        )

    def total_arrived(peer):
        return pltpu.make_async_remote_copy(
            src_ref=reduced,
            dst_ref=total.at[peer],
            send_sem=total_send.at[peer],
            recv_sem=total_recv.at[peer],
            device_id=(peer, c),
            device_id_type=MESH,
        )

    def peers(action):
        for peer in range(row_count):
            @pl.when(peer != r)
            def _():
                action(peer)

    step = 256 if cells % 256 == 0 else BLK
    half = row_count // 2
    group_rows = half * slice_rows
    inner[...] = jnp.zeros_like(inner)

    for turn in range(2):
        first = lax.rem(r // half + turn, 2) * half
        for at in range(half):
            @pl.when(first + at != r)
            def _():
                row_arrived(first + at).wait_recv()

            @pl.when(first + at == r)
            def _():
                for offset in range(col_count):
                    source = near(offset)
                    for k in range(ratio):
                        @pl.when(source * ratio + k == r)
                        def _():
                            row_local(stage if offset else slots_ref, source, k).wait()

        group = pl.ds(pl.multiple_of(first * slice_rows, group_rows), group_rows)

        @pl.loop(0, cells // step)
        def _(i):
            at = pl.ds(pl.multiple_of(i * step, step), step)
            block = picked[pl.ds(first, half), :, at].reshape(group_rows, step)
            inner[group, :] += jnp.dot(
                block, own_ref[at, :], precision=lax.Precision.HIGHEST, preferred_element_type=jnp.float32
            )

        for at in range(half):
            @pl.when(first + at != r)
            def _():
                part_copy(first + at).start()

    peers(lambda peer: part_arrived(peer).wait_recv())
    mine = inner[pl.ds(pl.multiple_of(r * slice_rows, slice_rows), slice_rows), :]
    for peer in range(row_count):
        @pl.when(peer == r)
        def _():
            part[peer] = mine
    value = part[0]
    for peer in range(1, row_count):
        value = value + part[peer]
    reduced[...] = value
    peers(lambda peer: total_copy(peer).start())

    @pl.loop(0, cells // step)
    def _(i):
        at = pl.ds(pl.multiple_of(i * step, step), step)
        block = picked[:, :, at].reshape(row_count * slice_rows, step)
        lower_ref[at, :] = block.T

    peers(lambda peer: total_arrived(peer).wait_recv())
    for peer in range(row_count):
        @pl.when(peer == r)
        def _():
            total[peer] = reduced[...]
    base = jnp.where(owner_ref[c] >= 0, base_ref[...], jnp.zeros_like(base_ref))
    diag_ref[...] = base - total[...].reshape(diag_ref.shape)

    for offset in range(col_count):
        source = near(offset)
        held = stage if offset else slots_ref
        if offset:
            for k in range(ratio):
                column_copy(source, k).wait_send()
        for k in range(ratio):
            @pl.when(source * ratio + k != r)
            def _():
                row_copy(held, source, k).wait_send()
    peers(lambda peer: part_copy(peer).wait_send())
    peers(lambda peer: total_copy(peer).wait_send())


def finish(owner, slots, own, base, row_count):
    col_count, slice_rows, _ = slots.shape
    cells, width = own.shape
    vmem = pl.BlockSpec(memory_space=pltpu.VMEM)
    dma = pltpu.SemaphoreType.DMA
    return pl.pallas_call(
        functools.partial(finish_kernel, row_count, col_count),
        out_shape=(
            jax.ShapeDtypeStruct((cells, width), jnp.float32),
            jax.ShapeDtypeStruct((width, width), jnp.float32),
        ),
        in_specs=[pl.BlockSpec(memory_space=pltpu.SMEM)] + [vmem] * 3,
        out_specs=(vmem, vmem),
        scratch_shapes=[
            pltpu.VMEM(slots.shape, jnp.float32),
            pltpu.VMEM((row_count, slice_rows, cells), jnp.float32),
            pltpu.VMEM((width, width), jnp.float32),
            pltpu.VMEM((row_count, slice_rows, width), jnp.float32),
            pltpu.VMEM((slice_rows, width), jnp.float32),
            pltpu.VMEM((row_count, slice_rows, width), jnp.float32),
            dma((col_count, row_count // col_count)),
            dma((col_count, row_count // col_count)),
            dma((row_count,)),
            dma((row_count,)),
            dma((row_count,)),
            dma((row_count,)),
            dma((row_count,)),
            dma((row_count,)),
        ],
        compiler_params=pltpu.CompilerParams(collective_id=0, has_side_effects=True),
    )(owner, slots, own, base)


def per_device(anc_inverse, l_store, diag_inv, block_lists, block_counts, sibling_columns):
    siblings = block_lists.shape[0]
    row_count, col_count = lax.axis_size("row"), lax.axis_size("col")
    r, c = lax.axis_index("row"), lax.axis_index("col")
    row_blocks, col_blocks = anc_inverse.shape[0] // BLK, anc_inverse.shape[1] // BLK
    pairs = col_count // 2
    mate = [(k, k + 1 - 2 * (k % 2)) for k in range(col_count)]
    panel = l_store[0]
    near = [panel, lax.ppermute(panel, "col", mate)]
    moved = [
        lax.ppermute(panel, "col", [(k, (k + 2 * step) % col_count) for k in range(col_count)])
        for step in range(1, pairs)
    ]

    table = listed_table(block_lists, block_counts, row_blocks * row_count)
    row_listed = lax.dynamic_slice_in_dim(table, r * row_blocks, row_blocks, axis=1)
    col_listed = lax.dynamic_slice_in_dim(table, c * col_blocks, col_blocks, axis=1)
    row_ints = row_listed.astype(jnp.int32)
    counts = jnp.sum(row_ints, axis=1)
    place = jnp.cumsum(row_ints, axis=1) - 1
    ids = jnp.arange(row_blocks, dtype=jnp.int32)
    entry = jnp.arange(-(-row_blocks // GROUP) * GROUP, dtype=jnp.int32)
    hits = row_listed[:, :, None] & (place[:, :, None] == entry[None, None, :])
    rows = jnp.sum(jnp.where(hits, ids[None, :, None], 0), axis=1).astype(jnp.int32)

    flat = col_listed.reshape(-1)
    slot = jnp.where(flat, jnp.cumsum(flat.astype(jnp.int32)) - 1, -1).astype(jnp.int32)
    per_column = jnp.sum(table.reshape(siblings, col_count, col_blocks).astype(jnp.int32), axis=(0, 2))
    needed = jnp.max(per_column)
    slots_all = -(-siblings * col_blocks // 40) * 40
    grain = slots_all // 40
    caps = [grain * n for n in (19, 21, 23, 25, 28, 32, 40)]
    level = jnp.sum((needed > jnp.array(caps[:-1], jnp.int32)).astype(jnp.int32))

    match = sibling_columns[:, None] == jnp.arange(col_count, dtype=jnp.int32)[None, :]
    owner = jnp.max(
        jnp.where(match, jnp.arange(siblings, dtype=jnp.int32)[:, None], -1), axis=0
    ).astype(jnp.int32)
    slot_rows = slot.reshape(siblings, col_blocks)

    def tables(columns):
        owned = (sibling_columns[None, :] == jnp.stack(columns)[:, None]).astype(jnp.int32)
        return (
            jnp.sum(owned[:, :, None] * (slot_rows + 1)[None], axis=1) - 1,
            jnp.sum(owned[:, :, None] * rows[None], axis=1),
            jnp.sum(owned * counts[None, :], axis=1),
        )

    mate_of = c + 1 - 2 * (c % 2)
    near_columns = [c, mate_of]
    far_columns = []
    for step in range(1, pairs):
        far_columns += [lax.rem(c - 2 * step + col_count, col_count), lax.rem(mate_of - 2 * step + col_count, col_count)]
    partial_value, high, low = product(*tables(near_columns), anc_inverse, near, slots_all)
    if moved:
        moved, partial_value = lax.optimization_barrier((moved, partial_value))
        far = [panel for one in moved for panel in (one, lax.ppermute(one, "col", mate))]
        partial_value = product(*tables(far_columns), anc_inverse, far, slots_all, (partial_value, high, low))

    def branch(place, cap):
        def run(value):
            compact = reduce_rows(value, row_count, cap // grain, grain * BLK, place + 1)
            return expand(slot, owner, compact, siblings, col_blocks)
        return run

    upper, slots = lax.switch(level, [branch(place, cap) for place, cap in enumerate(caps)], partial_value)
    lower, diag = finish(owner, slots, l_store[0], diag_inv[0], row_count)
    return upper, lower[None], diag[None]


def solution(mesh):
    return jax.shard_map(
        per_device,
        mesh=mesh,
        in_specs=(P("row", "col"), P("col", "row", None), P("col", None, None), P(), P(), P()),
        out_specs=(P(None, "row", "col"), P("col", "row", None), P("col", None, None)),
        check_vma=False,
    )
```

profile of v0, /device:TPU:0, one launch (start us, length us, event | category | flops | bytes accessed | tf_op | source)
XLA Modules:
  0.0 332.4 jit_solution(679700387400516099)
XLA Ops:
  0.6 3.0 collective-permute-start
  3.7 0.7 iota_compare_fusion.3
  4.4 0.9 fusion.1
  5.5 0.3 reduce-window.9
  6.2 0.2 convert_reduce_fusion.1
  6.4 0.2 reduce_window_sum.28
  6.7 0.7 compare_convert_fusion.1
  7.8 0.6 sub.32.slot_ref
  8.6 0.6 reshape.157.rows_ref
  9.2 1.4 fusion.5
  10.5 42.7 %shard_map.94 = (f32[256,20480]{1,0:T(8,128)}, bf16[4,20,128,1024]{3,2,1,0:T(8,128)(2,1)}, bf16[4,20,128,1024]{3,2,1,0:T(8,128)(2,1)}) custom-call(s32[80]{0:T(128)} %sub.32.slot_ref, s32[40]{0:T(128)} %reshape.157.rows_ref, s32[2]{0:T(128)} %get-tuple-element.88.count_ref, f32[2560,5120]{1,0:T(8,128)} %a_ref.3, f32[2560,256]{1,0:T(8,128)} %bitcast.28, ...), custom_call_target="tpu_custom_call" | custom-call | flops 20132659200 | bytes 62914560 | tf_op jit(solution)/shard_map/pallas_call | solution.py:182
  53.2 7.6 %collective-permute-done.refs_0_ = f32[2560,256]{1,0:T(8,128)} collective-permute-done((f32[2560,256]{1,0:T(8,128)}, f32[2560,256]{1,0:T(8,128)}, u32[]{:S(2)}, u32[]{:S(2)}) %collective-permute-start) | collective-permute-done | bytes 2621472 | tf_op jit(solution)/shard_map/ppermute | solution.py:734
  61.1 0.6 sub.29.slot_ref
  61.7 0.7 reshape.156.rows_ref
  62.3 0.6 reduce_max.18
  63.0 1.3 fusion.6
  65.0 1.1 collective-permute-done.2.refs_1_
  66.1 40.7 %shard_map.95 = f32[256,20480]{1,0:T(8,128)} custom-call(s32[80]{0:T(128)} %sub.29.slot_ref, s32[40]{0:T(128)} %reshape.156.rows_ref, s32[2]{0:T(128)} %get-tuple-element.89.count_ref, f32[2560,5120]{1,0:T(8,128)} %a_ref.3, f32[2560,256]{1,0:T(8,128)} %collective-permute-done.refs_0_, ...), custom_call_target="tpu_custom_call", output_to_operand_aliasing={{}: (6, {})} | custom-call | flops 20132659200 | bytes 62914560 | tf_op jit(solution)/shard_map/pallas_call | solution.py:182
  106.8 126.9 %conditional.1 = ((f32[4,32,5120]{2,1,0:T(8,128)}, f32[4,32,5120]{2,1,0:T(8,128)S(1)})) conditional(s32[]{:T(128)} %clamp.3, (f32[256,20480]{1,0:T(8,128)}, s32[160]{0:T(256)S(1)}, s32[4]{0:T(128)S(1)}) %tuple.31, (f32[256,20480]{1,0:T(8,128)}, s32[160]{0:T(256)S(1)}, s32[4]{0:T(128)S(1)}) %tuple.31, ...), branch_computations={%region_17.18_spmd, %region_18.19_spmd, %region_19.20_spmd, %regio... | conditional | bytes 8 | solution.py:789
  106.8 122.9 %branch_1_fun.2.compact_ref = f32[32,10752]{1,0:T(8,128)} custom-call(f32[4,2,32,20480]{3,2,1,0:T(8,128)} %bitcast.20), custom_call_target="tpu_custom_call" | custom-call | tf_op jit(solution)/shard_map/cond/branch_1_fun/pallas_call | solution.py:447
  229.8 3.9 %branch_1_fun.3 = (f32[4,32,5120]{2,1,0:T(8,128)}, f32[4,32,5120]{2,1,0:T(8,128)S(1)}) custom-call(s32[160]{0:T(256)S(1)} %get-tuple-element.45.slot_ref, s32[4]{0:T(128)S(1)} %get-tuple-element.46.owner_ref, f32[32,10752]{1,0:T(8,128)} %branch_1_fun.2.compact_ref), custom_call_target="tpu_custom_call" | custom-call | tf_op jit(solution)/shard_map/cond/branch_1_fun/pallas_call | solution.py:233
  233.7 94.6 %shard_map.96 = (f32[2560,256]{1,0:T(8,128)}, f32[256,256]{1,0:T(8,128)}) custom-call(s32[4]{0:T(128)S(1)} %select_reduce_fusion.1.owner_ref, f32[4,32,5120]{2,1,0:T(8,128)S(1)} %get-tuple-element.81.slots_ref, f32[2560,256]{1,0:T(8,128)} %bitcast.29, f32[256,256]{1,0:T(8,128)} %bitcast.31), custom_call_target="tpu_custom_call" | custom-call | tf_op jit(solution)/shard_map/pallas_call | solution.py:696
  328.3 3.4 %copy.30 = f32[1,2560,256]{2,1,0:T(8,128)} copy(f32[1,2560,256]{2,1,0:T(8,128)} %bitcast.30) | data formatting | bytes 5242880
  331.7 0.7 copy.31
  (33 shorter events, 1.6 us)
Async XLA Ops:
  0.6 60.2 %collective-permute-start = (f32[2560,256]{1,0:T(8,128)}, f32[2560,256]{1,0:T(8,128)}, u32[]{:S(2)}, u32[]{:S(2)}) collective-permute-start(f32[2560,256]{1,0:T(8,128)} %bitcast.26), channel_id=1, source_target_pairs={{0,2},{1,3},{2,0},{3,1},{4,6},{5,7},{6,4},{7,5},{8,10},{9,11},{10,... | collective-permute-start | bytes 7864328 | tf_op jit(solution)/shard_map/ppermute | solution.py:734
  3.7 6.9 %collective-permute-start.1 = (f32[2560,256]{1,0:T(8,128)}, f32[2560,256]{1,0:T(8,128)}, u32[]{:S(2)}, u32[]{:S(2)}) collective-permute-start(f32[2560,256]{1,0:T(8,128)} %bitcast.27), channel_id=1, source_target_pairs={{0,1},{1,0},{2,3},{3,2},{4,5},{5,4},{6,7},{7,6},{8,9},{9,8},{10,11... | collective-permute-start | bytes 7864328 | tf_op jit(solution)/shard_map/ppermute | solution.py:732
  10.5 52.4 %copy-start.2 = (s32[6]{0:T(128)S(1)}, s32[6]{0:T(128)}, u32[]{:S(2)}) copy-start(s32[6]{0:T(128)} %constant.67.clone) | copy-start | bytes 76
  10.5 54.4 %copy-start.1 = (s32[4]{0:T(128)S(1)}, s32[4]{0:T(128)}, u32[]{:S(2)}) copy-start(s32[4]{0:T(128)} %param.19) | copy-start | bytes 52
  60.8 5.3 %collective-permute-start.2 = (f32[2560,256]{1,0:T(8,128)}, f32[2560,256]{1,0:T(8,128)}, u32[]{:S(2)}, u32[]{:S(2)}) collective-permute-start(f32[2560,256]{1,0:T(8,128)} %collective-permute-done.refs_0_), channel_id=1, source_target_pairs={{0,1},{1,0},{2,3},{3,2},{4,5},{5,4},{6,7},{7,6},{8,9},{9,8},{10,11... | collective-permute-start | bytes 7864328 | tf_op jit(solution)/shard_map/ppermute | solution.py:780
  328.3 3.5 %copy-start = (f32[256,256]{1,0:T(8,128)S(1)}, f32[256,256]{1,0:T(8,128)}, u32[]{:S(2)}) copy-start(f32[256,256]{1,0:T(8,128)} %get-tuple-element.83) | copy-start | bytes 786436
where the time goes:
time: 337 us; the launch traced here: 332 us
  Pallas kernels  305 us (91%)
  waiting for transfers between devices  8.73 us (3%)
  local copies, waits for them, and re-layouts  7.33 us (2%)
  other arithmetic  7.14 us (2%)
    pallas_call x1, Pallas kernels, reduce_rows(): pl.pallas_call(functools.partial(reduce_kernel, line, flat_first, chunks)...  123 us
    pallas_call x1, Pallas kernels, finish(): pl.pallas_call(functools.partial(finish_kernel, row_count, col_count), ou...  94.6 us
    pallas_call x2, Pallas kernels, product(): pl.pallas_call(functools.partial(product_kernel, members, tile_blocks, co...  83.4 us
    ppermute x1, waiting for transfers between devices, per_device(): lax.ppermute(panel, 'col', [(k, (k + 2 * step) % col_count) for k in rang...  7.62 us
  transfers between devices with their start and end apart: 3, of which 2 were waited for; matrix products, arithmetic and copies ran while one was open for 3% of the time, Pallas kernels for 13%

commit v1 on v0

--- a/solution.py
+++ b/solution.py
@@ -211,7 +211,7 @@
     )(slot.reshape(-1), rows.reshape(-1), counts, anc, *panels, *joins)
 
 
-def expand_kernel(siblings, col_count, col_blocks, slot_ref, owner_ref, compact_ref, upper_ref, slots_ref):
+def expand_kernel(siblings, col_count, ratio, col_blocks, slot_ref, owner_ref, compact_ref, upper_ref, slots_ref):
     @pl.loop(0, col_blocks)
     def _(block):
         lanes = pl.ds(pl.multiple_of(block * BLK, BLK), BLK)
@@ -221,20 +221,36 @@
             value = compact_ref[:, at]
             upper_ref[sibling, :, lanes] = jnp.where(slot >= 0, value, jnp.zeros_like(value))
 
+    blocks = col_blocks // ratio
     for column in range(col_count):
         sibling = owner_ref[column]
-        value = upper_ref[jnp.maximum(sibling, 0)]
-        slots_ref[column] = jnp.where(sibling >= 0, value, jnp.zeros_like(value))
-
-
-def expand(slot, owner, compact, siblings, col_blocks):
+        for k in range(ratio):
+            def pack(block, taken):
+                slot = jnp.where(sibling >= 0, slot_ref[jnp.maximum(sibling, 0) * col_blocks + k * blocks + block], -1)
+
+                @pl.when(slot >= 0)
+                def _():
+                    at = pl.ds(pl.multiple_of(slot * BLK, BLK), BLK)
+                    slots_ref[column, k, :, pl.ds(pl.multiple_of(taken * BLK, BLK), BLK)] = compact_ref[:, at]
+
+                return taken + (slot >= 0).astype(jnp.int32)
+
+            taken = lax.fori_loop(0, blocks, pack, jnp.int32(0))
+
+            @pl.loop(taken, blocks)
+            def _(block):
+                lanes = pl.ds(pl.multiple_of(block * BLK, BLK), BLK)
+                slots_ref[column, k, :, lanes] = jnp.zeros((slots_ref.shape[2], BLK), jnp.float32)
+
+
+def expand(slot, owner, compact, siblings, col_blocks, ratio):
     col_count = owner.shape[0]
     rows = compact.shape[0]
     return pl.pallas_call(
-        functools.partial(expand_kernel, siblings, col_count, col_blocks),
+        functools.partial(expand_kernel, siblings, col_count, ratio, col_blocks),
         out_shape=(
             jax.ShapeDtypeStruct((siblings, rows, col_blocks * BLK), jnp.float32),
-            jax.ShapeDtypeStruct((col_count, rows, col_blocks * BLK), jnp.float32),
+            jax.ShapeDtypeStruct((col_count, ratio, rows, col_blocks // ratio * BLK), jnp.float32),
         ),
         in_specs=[pl.BlockSpec(memory_space=pltpu.SMEM)] * 2 + [pl.BlockSpec(memory_space=pltpu.VMEM)],
         out_specs=(pl.BlockSpec(memory_space=pltpu.VMEM),) * 2,
@@ -476,8 +492,47 @@
     )(value.reshape(line, 2, slice_rows, columns))
 
 
+def pack_kernel(rows_ref, own_ref, out_ref):
+    @pl.loop(0, out_ref.shape[0] // BLK)
+    def _(block):
+        rows = pl.ds(pl.multiple_of(rows_ref[block] * BLK, BLK), BLK)
+        out_ref[pl.ds(pl.multiple_of(block * BLK, BLK), BLK), :] = own_ref[rows, :]
+
+
+def packed(rows, own):
+    vmem = pl.BlockSpec(memory_space=pltpu.VMEM)
+    return pl.pallas_call(
+        pack_kernel,
+        out_shape=jax.ShapeDtypeStruct(own.shape, own.dtype),
+        in_specs=[pl.BlockSpec(memory_space=pltpu.SMEM), vmem],
+        out_specs=vmem,
+    )(rows, own)
+
+
+def unpack_kernel(place_ref, picked_ref, lower_ref):
+    place = place_ref[pl.program_id(0)]
+    at = pl.ds(pl.multiple_of(jnp.maximum(place, 0) * BLK, BLK), BLK)
+    value = picked_ref[:, :, at].reshape(lower_ref.shape[1], BLK)
+    lower_ref[...] = jnp.where(place >= 0, value, jnp.zeros_like(value)).T
+
+
+def unpacked(place, picked, depth):
+    row_count, slice_rows, _ = picked.shape
+    width = row_count * slice_rows
+    return pl.pallas_call(
+        unpack_kernel,
+        out_shape=jax.ShapeDtypeStruct((depth, width), picked.dtype),
+        grid_spec=pltpu.PrefetchScalarGridSpec(
+            num_scalar_prefetch=1,
+            grid=(depth // BLK,),
+            in_specs=[pl.BlockSpec(picked.shape, lambda i, *_: (0, 0, 0), pipeline_mode=pl.Buffered(1))],
+            out_specs=pl.BlockSpec((BLK, width), lambda i, *_: (i, 0)),
+        ),
+    )(place, picked)
+
+
 def finish_kernel(row_count, col_count,
-                  owner_ref, slots_ref, own_ref, base_ref, lower_ref, diag_ref,
+                  owner_ref, slots_ref, own_ref, base_ref, picked_ref, diag_ref,
                   stage, picked, inner, part, reduced, total,
                   stage_send, stage_recv, send_sem, recv_sem, part_send, part_recv, total_send, total_recv):
     r, c = lax.axis_index("row"), lax.axis_index("col")
@@ -499,13 +554,12 @@
         pair = lax.rem(c // 2 + offset // 2, col_count // 2)
         return pair * 2 + lax.rem(lax.rem(c, 2) + offset % 2, 2)
 
-    def piece(k):
-        return pl.ds(k * cells, cells)
+    front = pl.ds(0, cells)
 
     def column_copy(target, k):
         return pltpu.make_async_remote_copy(
-            src_ref=slots_ref.at[target, :, piece(k)],
-            dst_ref=stage.at[c, :, piece(k)],
+            src_ref=slots_ref.at[target, k, :, front],
+            dst_ref=stage.at[c, k],
             send_sem=stage_send.at[target, k],
             recv_sem=stage_recv.at[c, k],
             device_id=(r, target),
@@ -514,8 +568,8 @@
 
     def column_arrived(source, k):
         return pltpu.make_async_remote_copy(
-            src_ref=slots_ref.at[source, :, piece(k)],
-            dst_ref=stage.at[source, :, piece(k)],
+            src_ref=slots_ref.at[source, k, :, front],
+            dst_ref=stage.at[source, k],
             send_sem=stage_send.at[source, k],
             recv_sem=stage_recv.at[source, k],
             device_id=(r, source),
@@ -525,7 +579,7 @@
     def row_copy(held, source, k):
         target = source * ratio + k
         return pltpu.make_async_remote_copy(
-            src_ref=held.at[source, :, piece(k)],
+            src_ref=held.at[source, k, :, front],
             dst_ref=picked.at[r],
             send_sem=send_sem.at[target],
             recv_sem=recv_sem.at[r],
@@ -535,7 +589,7 @@
 
     def row_local(held, source, k):
         return pltpu.make_async_copy(
-            held.at[source, :, piece(k)], picked.at[r], recv_sem.at[r]
+            held.at[source, k, :, front], picked.at[r], recv_sem.at[r]
         )
 
     def row_arrived(source):
@@ -660,11 +714,9 @@
     reduced[...] = value
     peers(lambda peer: total_copy(peer).start())
 
-    @pl.loop(0, cells // step)
-    def _(i):
-        at = pl.ds(pl.multiple_of(i * step, step), step)
-        block = picked[:, :, at].reshape(row_count * slice_rows, step)
-        lower_ref[at, :] = block.T
+    @pl.loop(0, row_count)
+    def _(source):
+        picked_ref[source] = picked[source]
 
     peers(lambda peer: total_arrived(peer).wait_recv())
     for peer in range(row_count):
@@ -688,21 +740,22 @@
     peers(lambda peer: total_copy(peer).wait_send())
 
 
-def finish(owner, slots, own, base, row_count):
-    col_count, slice_rows, _ = slots.shape
-    cells, width = own.shape
+def finish(owner, slots, own, base, row_count, most, collective):
+    col_count, ratio, slice_rows, _ = slots.shape
+    width = own.shape[1]
+    cells = most * BLK
     vmem = pl.BlockSpec(memory_space=pltpu.VMEM)
     dma = pltpu.SemaphoreType.DMA
     return pl.pallas_call(
         functools.partial(finish_kernel, row_count, col_count),
         out_shape=(
-            jax.ShapeDtypeStruct((cells, width), jnp.float32),
+            jax.ShapeDtypeStruct((row_count, slice_rows, cells), jnp.float32),
             jax.ShapeDtypeStruct((width, width), jnp.float32),
         ),
         in_specs=[pl.BlockSpec(memory_space=pltpu.SMEM)] + [vmem] * 3,
         out_specs=(vmem, vmem),
         scratch_shapes=[
-            pltpu.VMEM(slots.shape, jnp.float32),
+            pltpu.VMEM((col_count, ratio, slice_rows, cells), jnp.float32),
             pltpu.VMEM((row_count, slice_rows, cells), jnp.float32),
             pltpu.VMEM((width, width), jnp.float32),
             pltpu.VMEM((row_count, slice_rows, width), jnp.float32),
@@ -717,7 +770,7 @@
             dma((row_count,)),
             dma((row_count,)),
         ],
-        compiler_params=pltpu.CompilerParams(collective_id=0, has_side_effects=True),
+        compiler_params=pltpu.CompilerParams(collective_id=collective, has_side_effects=True),
     )(owner, slots, own, base)
 
 
@@ -752,7 +805,7 @@
     needed = jnp.max(per_column)
     slots_all = -(-siblings * col_blocks // 40) * 40
     grain = slots_all // 40
-    caps = [grain * n for n in (19, 21, 23, 25, 28, 32, 40)]
+    caps = [grain * n for n in (19, 20, 21, 22, 23, 25, 28, 32, 40)]
     level = jnp.sum((needed > jnp.array(caps[:-1], jnp.int32)).astype(jnp.int32))
 
     match = sibling_columns[:, None] == jnp.arange(col_count, dtype=jnp.int32)[None, :]
@@ -774,7 +827,8 @@
     far_columns = []
     for step in range(1, pairs):
         far_columns += [lax.rem(c - 2 * step + col_count, col_count), lax.rem(mate_of - 2 * step + col_count, col_count)]
-    partial_value, high, low = product(*tables(near_columns), anc_inverse, near, slots_all)
+    near_tables = tables(near_columns)
+    partial_value, high, low = product(*near_tables, anc_inverse, near, slots_all)
     if moved:
         moved, partial_value = lax.optimization_barrier((moved, partial_value))
         far = [panel for one in moved for panel in (one, lax.ppermute(one, "col", mate))]
@@ -783,11 +837,28 @@
     def branch(place, cap):
         def run(value):
             compact = reduce_rows(value, row_count, cap // grain, grain * BLK, place + 1)
-            return expand(slot, owner, compact, siblings, col_blocks)
+            return expand(slot, owner, compact, siblings, col_blocks, row_count // col_count)
         return run
 
     upper, slots = lax.switch(level, [branch(place, cap) for place, cap in enumerate(caps)], partial_value)
-    lower, diag = finish(owner, slots, l_store[0], diag_inv[0], row_count)
+
+    own_rows = near_tables[1][0]
+    own_place = jnp.sum(
+        jnp.where(sibling_columns == c, 1, 0)[:, None] * jnp.where(row_listed, place + 1, 0), axis=0
+    ) - 1
+    most = jnp.max(jnp.sum(table.reshape(siblings, row_count, row_blocks).astype(jnp.int32), axis=2))
+    sizes = sorted({-(-row_blocks * n // 20) for n in (16, 18, 20)})
+    depth_level = jnp.sum((most > jnp.array(sizes[:-1], jnp.int32)).astype(jnp.int32))
+
+    def end(number, size):
+        def run(value, own, base):
+            picked, diag = finish(owner, value, own, base, row_count, size, len(caps) + 1 + number)
+            return unpacked(own_place, picked, own.shape[0]), diag
+        return run
+
+    lower, diag = lax.switch(
+        depth_level, [end(number, size) for number, size in enumerate(sizes)], slots, packed(own_rows, panel), diag_inv[0]
+    )
     return upper, lower[None], diag[None]
 
 

time: 337 us -> 323 us (0.958); the launches traced: 332 us -> 326 us
  Pallas kernels: 305 us -> 295 us
    pallas_call x1, Pallas kernels: 94.6 us -> 72.6 us  [finish(): pl.pallas_call(functools.partial(finish_kernel, row_count, col_count), ou...]
    pallas_call x1 -> x3, Pallas kernels: 3.9 us -> 14.8 us  [the longest x1 6.72 us: expand(): pl.pallas_call(functools.partial(expand_kernel, siblings, col_count, rati...]
  transfers between devices with their start and end apart: 3 -> 3, of which waited for: 2 -> 1; matrix products, arithmetic and copies ran while one was open for 3% -> 4% of each run, Pallas kernels for 13% -> 14%
where the time goes in v1:
time: 323 us; the launch traced here: 326 us
  Pallas kernels  295 us (91%)
  other arithmetic  9.98 us (3%)
  waiting for transfers between devices  9.85 us (3%)
  local copies, waits for them, and re-layouts  5.32 us (2%)
    pallas_call x1, Pallas kernels, reduce_rows(): pl.pallas_call(functools.partial(reduce_kernel, line, flat_first, chunks)...  124 us
    pallas_call x2, Pallas kernels, product(): pl.pallas_call(functools.partial(product_kernel, members, tile_blocks, co...  84.1 us
    pallas_call x1, Pallas kernels, finish(): pl.pallas_call(functools.partial(finish_kernel, row_count, col_count), ou...  72.6 us
    ppermute x1, waiting for transfers between devices, per_device(): lax.ppermute(panel, 'col', [(k, (k + 2 * step) % col_count) for k in rang...  9.85 us
    pallas_call x1, Pallas kernels, expand(): pl.pallas_call(functools.partial(expand_kernel, siblings, col_count, rati...  6.72 us
  transfers between devices with their start and end apart: 3, of which 1 were waited for; matrix products, arithmetic and copies ran while one was open for 4% of the time, Pallas kernels for 14%

profile of v1, /device:TPU:0, one launch (start us, length us, event | category | flops | bytes accessed | tf_op | source)
XLA Modules:
  0.0 325.5 jit_solution(1760161418337287565)
XLA Ops:
  1.2 2.6 collective-permute-start
  3.7 0.7 iota_compare_fusion.3
  4.5 0.9 fusion.1
  7.0 0.7 compare_convert_fusion.1
  8.6 0.6 sub.44.slot_ref
  9.2 1.4 fusion.5
  10.7 41.0 %shard_map.103 = (f32[256,20480]{1,0:T(8,128)}, bf16[4,20,128,1024]{3,2,1,0:T(8,128)(2,1)}, bf16[4,20,128,1024]{3,2,1,0:T(8,128)(2,1)}) custom-call(s32[80]{0:T(128)} %sub.44.slot_ref, s32[40]{0:T(128)} %reshape.163.rows_ref, s32[2]{0:T(128)} %get-tuple-element.257.count_ref, f32[2560,5120]{1,0:T(8,128)} %a_ref.3, f32[2560,256]{1,0:T(8,128)} %bitcast.41, ...), custom_call_target="tpu_custom_call" | custom-call | flops 20132659200 | bytes 62914560 | tf_op jit(solution)/shard_map/pallas_call | solution.py:182
  51.7 9.8 %collective-permute-done.refs_0_ = f32[2560,256]{1,0:T(8,128)} collective-permute-done((f32[2560,256]{1,0:T(8,128)}, f32[2560,256]{1,0:T(8,128)}, u32[]{:S(2)}, u32[]{:S(2)}) %collective-permute-start) | collective-permute-done | bytes 2621472 | tf_op jit(solution)/shard_map/ppermute | solution.py:787
  61.5 0.6 reshape.162.rows_ref
  62.1 0.6 sub.41.slot_ref
  63.5 3.6 %shard_map.105 = f32[2560,256]{1,0:T(8,128)} custom-call(s32[20]{0:T(128)} %slice_bitcast_fusion.rows_ref, f32[2560,256]{1,0:T(8,128)} %bitcast.42), custom_call_target="tpu_custom_call" | custom-call | tf_op jit(solution)/shard_map/pallas_call | solution.py:504
  67.3 0.6 reduce_max.27
  67.9 0.6 reduce_max.29
  68.6 1.4 fusion.7
  70.6 1.3 fusion.6
  72.7 43.1 %shard_map.104 = f32[256,20480]{1,0:T(8,128)} custom-call(s32[80]{0:T(128)} %sub.41.slot_ref, s32[40]{0:T(128)} %reshape.162.rows_ref, s32[2]{0:T(128)} %get-tuple-element.258.count_ref, f32[2560,5120]{1,0:T(8,128)} %a_ref.3, f32[2560,256]{1,0:T(8,128)} %collective-permute-done.refs_0_, ...), custom_call_target="tpu_custom_call", output_to_operand_aliasing={{}: (6, {})} | custom-call | flops 20132659200 | bytes 62914560 | tf_op jit(solution)/shard_map/pallas_call | solution.py:182
  115.8 130.4 %conditional.2 = ((f32[4,32,5120]{2,1,0:T(8,128)}, f32[4,2,32,2560]{3,2,1,0:T(8,128)S(1)})) conditional(s32[]{:T(128)} %clamp.6, (f32[256,20480]{1,0:T(8,128)}, s32[160]{0:T(256)S(1)}, s32[4]{0:T(128)S(1)}) %tuple.52, (f32[256,20480]{1,0:T(8,128)}, s32[160]{0:T(256)S(1)}, s32[4]{0:T(128)S(1)}) %tuple.52, ...), branch_computations={%region_17.18_spmd, %region_18.19_spmd, %region_19.20_spmd, %regio... | conditional | bytes 8 | solution.py:843
  115.8 123.6 %branch_2_fun.4.compact_ref = f32[32,10752]{1,0:T(8,128)} custom-call(f32[4,2,32,20480]{3,2,1,0:T(8,128)} %bitcast.29), custom_call_target="tpu_custom_call" | custom-call | tf_op jit(solution)/shard_map/cond/branch_2_fun/pallas_call | solution.py:463
  239.5 6.7 %branch_2_fun.5 = (f32[4,32,5120]{2,1,0:T(8,128)}, f32[4,2,32,2560]{3,2,1,0:T(8,128)S(1)}) custom-call(s32[160]{0:T(256)S(1)} %get-tuple-element.181.slot_ref, s32[4]{0:T(128)S(1)} %get-tuple-element.182.owner_ref, f32[32,10752]{1,0:T(8,128)} %branch_2_fun.4.compact_ref), custom_call_target="tpu_custom_call" | custom-call | tf_op jit(solution)/shard_map/cond/branch_2_fun/pallas_call | solution.py:249
  246.2 77.8 %conditional.3 = (f32[256,256]{1,0:T(8,128)S(1)}, f32[1,2560,256]{2,1,0:T(8,128)S(1)}) conditional(s32[]{:T(128)} %clamp.7, (f32[1,256,256]{2,1,0:T(8,128)S(1)}, s32[4]{0:T(128)S(1)}, f32[4,2,32,2560]{3,2,1,0:T(8,128)S(1)}, f32[2560,256]{1,0:T(8,128)}, s32[]{:T(128)}, /*index=5*/s32[4]{0:T(128)S(1)}, s32[4,20]{1,0:T(4,128)S(1)}, ...), branch_computations={%region_29.31_spmd, %region_31.33_spmd, %region_33.35_spmd} | conditional | flops 248 | bytes 708 | solution.py:859
  246.2 72.6 %branch_0_fun.6 = (f32[8,32,2048]{2,1,0:T(8,128)}, f32[256,256]{1,0:T(8,128)S(1)}) custom-call(s32[4]{0:T(128)S(1)} %get-tuple-element.202.owner_ref, f32[4,2,32,2560]{3,2,1,0:T(8,128)S(1)} %get-tuple-element.203.slots_ref, f32[2560,256]{1,0:T(8,128)} %get-tuple-element.204.own_ref, f32[256,256]{1,0:T(8,128)S(1)} %bitcast.43), custom_call_target="tpu_custom_call" | custom-call | tf_op jit(solution)/shard_map/cond/branch_0_fun/pallas_call | solution.py:749
  319.4 4.5 %branch_0_fun.7 = f32[2560,256]{1,0:T(8,128)S(1)} custom-call(s32[20]{0:T(128)} %broadcast_add_fusion.place_ref, f32[8,32,2048]{2,1,0:T(8,128)} %get-tuple-element.211.picked_ref), custom_call_target="tpu_custom_call" | custom-call | tf_op jit(solution)/shard_map/cond/branch_0_fun/pallas_call | solution.py:522
  324.0 0.8 copy.40
  324.7 0.8 copy-done
  (48 shorter events, 4.8 us)
Async XLA Ops:
  0.6 10.1 %collective-permute-start.1 = (f32[2560,256]{1,0:T(8,128)}, f32[2560,256]{1,0:T(8,128)}, u32[]{:S(2)}, u32[]{:S(2)}) collective-permute-start(f32[2560,256]{1,0:T(8,128)} %bitcast.39), channel_id=1, source_target_pairs={{0,1},{1,0},{2,3},{3,2},{4,5},{5,4},{6,7},{7,6},{8,9},{9,8},{10,11... | collective-permute-start | bytes 7864328 | tf_op jit(solution)/shard_map/ppermute | solution.py:785
  1.2 60.3 %collective-permute-start = (f32[2560,256]{1,0:T(8,128)}, f32[2560,256]{1,0:T(8,128)}, u32[]{:S(2)}, u32[]{:S(2)}) collective-permute-start(f32[2560,256]{1,0:T(8,128)} %bitcast.40), channel_id=1, source_target_pairs={{0,2},{1,3},{2,0},{3,1},{4,6},{5,7},{6,4},{7,5},{8,10},{9,11},{10,... | collective-permute-start | bytes 7864328 | tf_op jit(solution)/shard_map/ppermute | solution.py:787
  61.5 11.1 %collective-permute-start.2 = (f32[2560,256]{1,0:T(8,128)}, f32[2560,256]{1,0:T(8,128)}, u32[]{:S(2)}, u32[]{:S(2)}) collective-permute-start(f32[2560,256]{1,0:T(8,128)} %collective-permute-done.refs_0_), channel_id=1, source_target_pairs={{0,1},{1,0},{2,3},{3,2},{4,5},{5,4},{6,7},{7,6},{8,9},{9,8},{10,11... | collective-permute-start | bytes 7864328 | tf_op jit(solution)/shard_map/ppermute | solution.py:834
  63.5 5.1 %copy-start.4 = (s32[2]{0:T(128)S(1)}, s32[2]{0:T(128)}, u32[]{:S(2)}) copy-start(s32[2]{0:T(128)} %constant.81.clone) | copy-start | bytes 28
  63.5 7.1 %copy-start.3 = (s32[8]{0:T(128)S(1)}, s32[8]{0:T(128)}, u32[]{:S(2)}) copy-start(s32[8]{0:T(128)} %constant.80.clone) | copy-start | bytes 100
  63.5 9.1 %copy-start.2 = (s32[4]{0:T(128)S(1)}, s32[4]{0:T(128)}, u32[]{:S(2)}) copy-start(s32[4]{0:T(128)} %param.25) | copy-start | bytes 52
  115.8 130.4 %copy-start.1 = (f32[1,256,256]{2,1,0:T(8,128)S(1)}, f32[1,256,256]{2,1,0:T(8,128)}, u32[]{:S(2)}) copy-start(f32[1,256,256]{2,1,0:T(8,128)} %param.22) | copy-start | bytes 786436
  324.0 1.6 copy-start

commit v2 on v1

--- a/solution.py
+++ b/solution.py
@@ -828,6 +828,7 @@
     for step in range(1, pairs):
         far_columns += [lax.rem(c - 2 * step + col_count, col_count), lax.rem(mate_of - 2 * step + col_count, col_count)]
     near_tables = tables(near_columns)
+    near_tables, own_packed = lax.optimization_barrier((near_tables, packed(near_tables[1][0], panel)))
     partial_value, high, low = product(*near_tables, anc_inverse, near, slots_all)
     if moved:
         moved, partial_value = lax.optimization_barrier((moved, partial_value))
@@ -842,7 +843,6 @@
 
     upper, slots = lax.switch(level, [branch(place, cap) for place, cap in enumerate(caps)], partial_value)
 
-    own_rows = near_tables[1][0]
     own_place = jnp.sum(
         jnp.where(sibling_columns == c, 1, 0)[:, None] * jnp.where(row_listed, place + 1, 0), axis=0
     ) - 1
@@ -857,7 +857,7 @@
         return run
 
     lower, diag = lax.switch(
-        depth_level, [end(number, size) for number, size in enumerate(sizes)], slots, packed(own_rows, panel), diag_inv[0]
+        depth_level, [end(number, size) for number, size in enumerate(sizes)], slots, own_packed, diag_inv[0]
     )
     return upper, lower[None], diag[None]
 

time: 323 us -> 324 us (level)
  Pallas kernels: 295 us -> 307 us
  waiting for transfers between devices: 9.85 us -> 0.01 us
    pallas_call x2, Pallas kernels: 84.1 us -> 95.2 us  [product(): pl.pallas_call(functools.partial(product_kernel, members, tile_blocks, co...]
    ppermute x1, waiting for transfers between devices: 9.85 us -> 0.01 us  [per_device(): lax.ppermute(panel, 'col', [(k, (k + 2 * step) % col_count) for k in rang...]
  transfers between devices with their start and end apart: 3 -> 3, of which waited for: 1 -> 0; matrix products, arithmetic and copies ran while one was open for 4% -> 4% of each run, Pallas kernels for 14% -> 17%
where the time goes in v2:
time: 324 us; the launch traced here: 327 us
  Pallas kernels  307 us (95%)
  other arithmetic  9.33 us (3%)
  local copies, waits for them, and re-layouts  5.35 us (2%)
  starting transfers between devices  3.32 us (1%)
    pallas_call x1, Pallas kernels, reduce_rows(): pl.pallas_call(functools.partial(reduce_kernel, line, flat_first, chunks)...  122 us
    pallas_call x2, Pallas kernels, product(): pl.pallas_call(functools.partial(product_kernel, members, tile_blocks, co...  95.2 us
    pallas_call x1, Pallas kernels, finish(): pl.pallas_call(functools.partial(finish_kernel, row_count, col_count), ou...  75.2 us
    pallas_call x1, Pallas kernels, expand(): pl.pallas_call(functools.partial(expand_kernel, siblings, col_count, rati...  6.72 us
  transfers between devices with their start and end apart: 3, of which 0 were waited for; matrix products, arithmetic and copies ran while one was open for 4% of the time, Pallas kernels for 17%

profile of v2, /device:TPU:0, one launch (start us, length us, event | category | flops | bytes accessed | tf_op | source)
XLA Modules:
  0.0 327.2 jit_solution(5166606313344902411)
XLA Ops:
  1.2 2.6 collective-permute-start
  3.7 0.7 iota_compare_fusion.3
  4.5 0.9 fusion.1
  6.9 0.7 compare_convert_fusion.1
  8.3 3.5 %shard_map.103 = f32[2560,256]{1,0:T(8,128)} custom-call(s32[20]{0:T(128)} %slice_bitcast_fusion.rows_ref, f32[2560,256]{1,0:T(8,128)} %bitcast.41), custom_call_target="tpu_custom_call" | custom-call | tf_op jit(solution)/shard_map/pallas_call | solution.py:504
  11.9 0.8 fusion.5
  12.9 0.6 reshape.162.slot_ref
  13.5 0.6 reshape.163.rows_ref
  14.1 51.4 %shard_map.104 = (f32[256,20480]{1,0:T(8,128)}, bf16[4,20,128,1024]{3,2,1,0:T(8,128)(2,1)}, bf16[4,20,128,1024]{3,2,1,0:T(8,128)(2,1)}) custom-call(s32[80]{0:T(128)} %reshape.162.slot_ref, s32[40]{0:T(128)} %reshape.163.rows_ref, s32[2]{0:T(128)} %get-tuple-element.250.count_ref, f32[2560,5120]{1,0:T(8,128)} %a_ref.3, f32[2560,256]{1,0:T(8,128)} %bitcast.42, ...), custom_call_target="tpu_custom_call" | custom-call | flops 20132659200 | bytes 62914560 | tf_op jit(solution)/shard_map/pallas_call | solution.py:182
  65.8 0.6 reshape.161.rows_ref
  66.4 0.6 sub.39.slot_ref
  67.4 0.6 reduce_max.27
  68.1 0.6 reduce_max.29
  68.7 1.4 fusion.7
  70.8 1.3 fusion.6
  72.8 43.8 %shard_map.105 = f32[256,20480]{1,0:T(8,128)} custom-call(s32[80]{0:T(128)} %sub.39.slot_ref, s32[40]{0:T(128)} %reshape.161.rows_ref, s32[2]{0:T(128)} %get-tuple-element.266.count_ref, f32[2560,5120]{1,0:T(8,128)} %a_ref.3, f32[2560,256]{1,0:T(8,128)} %collective-permute-done.refs_0_, ...), custom_call_target="tpu_custom_call", output_to_operand_aliasing={{}: (6, {})} | custom-call | flops 20132659200 | bytes 62914560 | tf_op jit(solution)/shard_map/pallas_call | solution.py:182
  116.6 128.7 %conditional.2 = ((f32[4,32,5120]{2,1,0:T(8,128)}, f32[4,2,32,2560]{3,2,1,0:T(8,128)S(1)})) conditional(s32[]{:T(128)} %clamp.6, (f32[256,20480]{1,0:T(8,128)}, s32[160]{0:T(256)S(1)}, s32[4]{0:T(128)S(1)}) %tuple.54, (f32[256,20480]{1,0:T(8,128)}, s32[160]{0:T(256)S(1)}, s32[4]{0:T(128)S(1)}) %tuple.54, ...), branch_computations={%region_17.18_spmd, %region_18.19_spmd, %region_19.20_spmd, %regio... | conditional | bytes 8 | solution.py:844
  116.7 121.9 %branch_3_fun.2.compact_ref = f32[32,11264]{1,0:T(8,128)} custom-call(f32[4,2,32,20480]{3,2,1,0:T(8,128)} %bitcast.30), custom_call_target="tpu_custom_call" | custom-call | tf_op jit(solution)/shard_map/cond/branch_3_fun/pallas_call | solution.py:463
  238.6 6.7 %branch_3_fun.3 = (f32[4,32,5120]{2,1,0:T(8,128)}, f32[4,2,32,2560]{3,2,1,0:T(8,128)S(1)}) custom-call(s32[160]{0:T(256)S(1)} %get-tuple-element.184.slot_ref, s32[4]{0:T(128)S(1)} %get-tuple-element.185.owner_ref, f32[32,11264]{1,0:T(8,128)} %branch_3_fun.2.compact_ref), custom_call_target="tpu_custom_call" | custom-call | tf_op jit(solution)/shard_map/cond/branch_3_fun/pallas_call | solution.py:249
  245.3 80.3 %conditional.3 = (f32[256,256]{1,0:T(8,128)S(1)}, f32[1,2560,256]{2,1,0:T(8,128)S(1)}) conditional(s32[]{:T(128)} %clamp.7, (f32[1,256,256]{2,1,0:T(8,128)S(1)}, s32[4]{0:T(128)S(1)}, f32[4,2,32,2560]{3,2,1,0:T(8,128)S(1)}, f32[2560,256]{1,0:T(8,128)}, s32[]{:T(128)}, /*index=5*/s32[4]{0:T(128)S(1)}, s32[4,20]{1,0:T(4,128)S(1)}, ...), branch_computations={%region_29.31_spmd, %region_31.33_spmd, %region_33.35_spmd} | conditional | flops 248 | bytes 708 | solution.py:859
  245.3 75.2 %branch_0_fun.6 = (f32[8,32,2048]{2,1,0:T(8,128)}, f32[256,256]{1,0:T(8,128)S(1)}) custom-call(s32[4]{0:T(128)S(1)} %get-tuple-element.202.owner_ref, f32[4,2,32,2560]{3,2,1,0:T(8,128)S(1)} %get-tuple-element.203.slots_ref, f32[2560,256]{1,0:T(8,128)} %get-tuple-element.204.own_ref, f32[256,256]{1,0:T(8,128)S(1)} %bitcast.43), custom_call_target="tpu_custom_call" | custom-call | tf_op jit(solution)/shard_map/cond/branch_0_fun/pallas_call | solution.py:749
  321.1 4.5 %branch_0_fun.7 = f32[2560,256]{1,0:T(8,128)S(1)} custom-call(s32[20]{0:T(128)} %broadcast_add_fusion.place_ref, f32[8,32,2048]{2,1,0:T(8,128)} %get-tuple-element.211.picked_ref), custom_call_target="tpu_custom_call" | custom-call | tf_op jit(solution)/shard_map/cond/branch_0_fun/pallas_call | solution.py:522
  325.7 0.8 copy.40
  326.4 0.8 copy-done
  (48 shorter events, 4.4 us)
Async XLA Ops:
  0.6 13.5 %collective-permute-start.1 = (f32[2560,256]{1,0:T(8,128)}, f32[2560,256]{1,0:T(8,128)}, u32[]{:S(2)}, u32[]{:S(2)}) collective-permute-start(f32[2560,256]{1,0:T(8,128)} %bitcast.39), channel_id=1, source_target_pairs={{0,1},{1,0},{2,3},{3,2},{4,5},{5,4},{6,7},{7,6},{8,9},{9,8},{10,11... | collective-permute-start | bytes 7864328 | tf_op jit(solution)/shard_map/ppermute | solution.py:785
  1.2 64.3 %collective-permute-start = (f32[2560,256]{1,0:T(8,128)}, f32[2560,256]{1,0:T(8,128)}, u32[]{:S(2)}, u32[]{:S(2)}) collective-permute-start(f32[2560,256]{1,0:T(8,128)} %bitcast.40), channel_id=1, source_target_pairs={{0,2},{1,3},{2,0},{3,1},{4,6},{5,7},{6,4},{7,5},{8,10},{9,11},{10,... | collective-permute-start | bytes 7864328 | tf_op jit(solution)/shard_map/ppermute | solution.py:787
  8.3 3.6 %copy-start.2 = (s32[4]{0:T(128)S(1)}, s32[4]{0:T(128)}, u32[]{:S(2)}) copy-start(s32[4]{0:T(128)} %param.25) | copy-start | bytes 52
  14.1 54.6 %copy-start.4 = (s32[2]{0:T(128)S(1)}, s32[2]{0:T(128)}, u32[]{:S(2)}) copy-start(s32[2]{0:T(128)} %constant.81.clone) | copy-start | bytes 28
  14.1 56.6 %copy-start.3 = (s32[8]{0:T(128)S(1)}, s32[8]{0:T(128)}, u32[]{:S(2)}) copy-start(s32[8]{0:T(128)} %constant.80.clone) | copy-start | bytes 100
  65.5 7.2 %collective-permute-start.2 = (f32[2560,256]{1,0:T(8,128)}, f32[2560,256]{1,0:T(8,128)}, u32[]{:S(2)}, u32[]{:S(2)}) collective-permute-start(f32[2560,256]{1,0:T(8,128)} %collective-permute-done.refs_0_), channel_id=1, source_target_pairs={{0,1},{1,0},{2,3},{3,2},{4,5},{5,4},{6,7},{7,6},{8,9},{9,8},{10,11... | collective-permute-start | bytes 7864328 | tf_op jit(solution)/shard_map/ppermute | solution.py:835
  116.6 128.7 %copy-start.1 = (f32[1,256,256]{2,1,0:T(8,128)S(1)}, f32[1,256,256]{2,1,0:T(8,128)}, u32[]{:S(2)}) copy-start(f32[1,256,256]{2,1,0:T(8,128)} %param.22) | copy-start | bytes 786436
  325.7 1.6 copy-start
